TPU v7x, 32 devices: a whole 2x2x4 slice. The times are simulated.
32 devices in a mesh: row: 8 (over y, x, core), col: 4 (over z).
Axes of the slice: x: 2, y: 2, z: 4, core: 2. Of those that a mesh axis runs over, the one named last changes fastest.
Arguments:
- inverse: float32 [20480, 20480], P('row', 'col'), may hold values from -6 to 6
- factor: float32 [20480, 2, 256], P(('row', 'col')), may hold values from -0.0390625 to 0.0390625
- diag_inverse: float32 [2, 256, 256], replicated, may hold values from -6 to 6
- block_sizes: int32 [64], replicated, may hold values from 1 to 1280, 20480 in all
- listed: int32 [2, 64], replicated, may hold values 0 or 1
Outputs:
- ancestor_rows: float32 [20480, 2, 256], P(('row', 'col'))
- diagonal_block: float32 [2, 256, 256], replicated
Inputs may be any that keep to these rules, and one draw needn't show every extreme that they name: `block_sizes`: positive sizes that sum to 20480; the largest is exactly 1280.
All inputs are finite; a program needn't handle non-finite values.
Results may differ from a plain program's by a relative error of at most 0.00007.
Values sent between devices are 32-bit elements; how exact they have to be, the bound alone decides.
A program may use at most 128 MiB of HBM per device.

v0:
```python
import jax
import jax.numpy as jnp
from jax import lax
from jax.sharding import PartitionSpec as P


def from_root(value, axis, source):
    kept = jnp.where(lax.axis_index(axis) == source, value, 0).astype(value.dtype)
    return lax.psum(kept, axis)


def membership(first_row, row_total, block_sizes, listed):
    block_ends = jnp.cumsum(block_sizes)
    block_starts = block_ends - block_sizes
    positions = first_row + jnp.arange(row_total, dtype=jnp.int32)
    inside = (
        (positions[:, None] >= block_starts[None, :]) & (positions[:, None] < block_ends[None, :])
    ).astype(jnp.float32)
    return jnp.dot(
        inside,
        listed.astype(jnp.float32).T,
        precision=lax.Precision.HIGHEST,
        preferred_element_type=jnp.float32,
    )


def per_device(inverse, factor, diag_inverse, block_sizes, listed):
    n_rowdev = lax.axis_size("row")
    n_coldev = lax.axis_size("col")
    row_place = lax.axis_index("row")
    col_place = lax.axis_index("col")
    shard_rows = factor.shape[0]
    sibling_count = factor.shape[1]
    width = factor.shape[2]
    ratio = n_rowdev // n_coldev
    row_block = lax.all_gather(factor, "col", axis=0, tiled=True)
    gathered = []
    for offset in range(ratio):
        gathered.append(from_root(row_block, "row", col_place * ratio + offset))
    col_block = jnp.concatenate(gathered, axis=0)
    col_rows = col_block.shape[0]
    col_member = membership(col_place * col_rows, col_rows, block_sizes, listed)
    panel = (col_block * col_member[:, :, None]).reshape(col_rows, sibling_count * width)
    block_total = inverse.shape[0]
    partial_value = -jnp.dot(
        inverse, panel, precision=lax.Precision.HIGHEST, preferred_element_type=jnp.float32
    )
    summed = lax.psum(partial_value, "col")
    block_member = membership(row_place * block_total, block_total, block_sizes, listed)
    block_result = summed.reshape(block_total, sibling_count, width) * block_member[:, :, None]
    schur_term = jnp.einsum(
        "isw,isv->swv", row_block, block_result, precision=lax.Precision.HIGHEST
    )
    schur = lax.psum(schur_term, "row")
    ancestor_rows = lax.dynamic_slice_in_dim(block_result, col_place * shard_rows, shard_rows, 0)
    return (ancestor_rows, diag_inverse - schur)


def solution(mesh):
    in_specs = (P("row", "col"), P(("row", "col"), None, None), P(), P(), P())
    out_specs = (P(("row", "col"), None, None), P())
    return jax.shard_map(
        per_device, mesh=mesh, in_specs=in_specs, out_specs=out_specs, check_vma=False
    )
```

profile of v0, /device:TPU:1, one launch (start us, length us, event | category | flops | bytes accessed | tf_op | source)
XLA Modules:
  0.0 652.5 jit_solution(9232629267015286627)
XLA Ops:
  7.2 0.0 all-gather.2.cloned.1.call-start
  7.2 2.5 copy.24
  9.7 0.0 all-gather.2.cloned.1.call-update
  9.7 0.0 all-reduce.9.cloned.1.call-start
  9.8 100.5 %all-gather.2.cloned.1.call-done = f32[2560,2,256]{2,0,1:T(8,128)} async-done(((f32[640,2,256]{2,0,1:T(8,128)}), f32[2560,2,256]{2,0,1:T(8,128)}) %all-gather.2.cloned.1.call-update) | async-done | bytes 5242896 | tf_op jit(solution)/shard_map/all_gather | solution.py:36
  110.3 7.2 %broadcast_select_fusion.1 = (f32[2560,2,256]{2,0,1:T(8,128)}, f32[2560,2,256]{2,0,1:T(8,128)}) fusion(f32[2560,2,256]{2,0,1:T(8,128)} %all-gather.2.cloned.1.call-done, pred[]{:T(512)S(6)} %eq.6, pred[]{:T(512)S(6)} %eq.7), kind=kLoop, calls=%fused_computation.9 | loop fusion | flops 2621440 | bytes 15728642 | tf_op jit(solution)/shard_map/jit(_where)/select_n | solution.py:8
  117.5 5.9 copy.25
  123.4 5.9 copy.26
  129.3 0.0 all-reduce.9.cloned.1.call-update
  129.3 0.0 all-reduce.5.cloned.1.call-start
  129.4 0.6 copy-done.3
  130.0 0.1 copy.27
  130.0 0.1 reduce-window.8
  130.1 0.1 reduce
  130.3 0.6 fusion.10
  130.9 145.7 %all-reduce.9.cloned.1.call-done = (f32[2560,512]{0,1:T(8,128)}, f32[2560,512]{0,1:T(8,128)}) async-done(((f32[2560,512]{0,1:T(8,128)}, f32[2560,512]{0,1:T(8,128)}), (f32[2560,512]{0,1:T(8,128)}, f32[2560,512]{0,1:T(8,128)})) %all-reduce.9.cloned.1.call-update) | async-done | bytes 10485776 | tf_op jit(solution)/shard_map/psum | solution.py:9
  276.6 5.2 mul.34
  281.8 91.4 %fusion.5 = f32[512,2560]{1,0:T(8,128)} fusion(f32[2560,5120]{1,0:T(8,128)} %param.5, f32[5120,512]{0,1:T(8,128)} %bitcast.14, f32[2560,512]{0,1:T(8,128)} %get-tuple-element.8, f32[2560,512]{0,1:T(8,128)} %get-tuple-element.9), kind=kOutput, calls=%fused_computation.6 | convolution fusion | flops 80537190400 | bytes 78643200 | tf_op jit(solution)/shard_map/dot_general | solution.py:45
  373.2 8.7 %copy.28 = f32[2560,2,256]{2,1,0:T(2,128)} copy(f32[2560,2,256]{0,2,1:T(8,128)} %bitcast.15) | data formatting | bytes 10485760 | tf_op jit(solution)/shard_map/reshape | solution.py:50
  382.0 0.0 all-reduce.5.cloned.1.call-update
  382.0 0.2 all-reduce.7.cloned.1.call-start
  382.2 0.9 fusion.6
  383.1 188.1 %all-reduce.5.cloned.1.call-done = f32[2560,2,256]{2,1,0:T(2,128)} async-done(((f32[2560,2,256]{2,1,0:T(2,128)}), f32[2560,2,256]{2,1,0:T(2,128)}) %all-reduce.5.cloned.1.call-update) | async-done | bytes 5242896 | tf_op jit(solution)/shard_map/psum | solution.py:48
  571.2 5.5 broadcast_multiply_fusion
  576.8 2.3 copy-done
  579.1 11.5 %fusion.11 = f32[2,256,256]{1,2,0:T(8,128)} fusion(f32[2560,2,256]{2,0,1:T(8,128)} %all-gather.2.cloned.1.call-done, f32[2560,2,256]{2,1,0:T(2,128)S(1)} %broadcast_multiply_fusion), kind=kOutput, calls=%fused_computation.16 | convolution fusion | flops 4026531840 | bytes 11010048 | tf_op jit(solution)/shard_map/isw,isv->swv/dot_general | solution.py:51
  590.5 0.0 all-reduce.7.cloned.1.call-update
  590.6 0.2 copy.31
  590.8 2.8 constant_dynamic-slice_fusion
  593.6 50.2 %all-reduce.7.cloned.1.call-done = f32[2,256,256]{1,2,0:T(8,128)} async-done(((f32[2,256,256]{1,2,0:T(8,128)}), f32[2,256,256]{1,2,0:T(8,128)}) %all-reduce.7.cloned.1.call-update) | async-done | bytes 524304 | tf_op jit(solution)/shard_map/psum | solution.py:54
  643.8 1.1 sub.8
  644.9 1.0 copy.32
  (9 shorter events, 0.0 us)
Async XLA Ops:
  7.2 103.1 %all-gather.2.cloned.1.call-start = ((), (), s32[]{:S(2)}) async-start(), calls=%async_computation | async-start | bytes 6553600 | tf_op jit(solution)/shard_map/all_gather | solution.py:36
  9.7 266.9 %all-reduce.9.cloned.1.call-start = ((), (), s32[]{:S(2)}) async-start(), calls=%async_computation.3 | async-start | bytes 20971520 | tf_op jit(solution)/shard_map/psum | solution.py:9
  129.3 0.7 copy-start.3
  129.3 1.0 copy-start.2
  129.3 441.9 %all-reduce.5.cloned.1.call-start = ((), (), s32[]{:S(2)}) async-start(), calls=%async_computation.1 | async-start | bytes 10485760 | tf_op jit(solution)/shard_map/psum | solution.py:48
  382.0 261.8 %all-reduce.7.cloned.1.call-start = ((), (), s32[]{:S(2)}) async-start(), calls=%async_computation.2 | async-start | bytes 1048576 | tf_op jit(solution)/shard_map/psum | solution.py:54
  576.8 2.3 copy-start
  579.1 11.5 %copy-start.1 = (f32[2,256,256]{2,1,0:T(8,128)S(1)}, f32[2,256,256]{2,1,0:T(8,128)}, u32[]{:S(2)}) copy-start(f32[2,256,256]{2,1,0:T(8,128)} %param.7) | copy-start | bytes 1572868
Sparse Core Ops, SparseCore 0:
  10.1 100.1 all-gather.1
  129.4 147.1 all-reduce.8
  382.1 189.0 all-reduce.4
  590.7 53.0 all-reduce.6
where the time goes:
time: 655 us; the launch traced here: 652 us
  waiting for transfers between devices  485 us (74%)
  matrix products  104 us (16%)
  local copies, waits for them, and re-layouts  35.2 us (5%)
  other arithmetic  14.1 us (2%)
  between operations  13.9 us (2%)
    psum x1, waiting for transfers between devices, per_device(): summed = lax.psum(partial_value, 'col')  188 us
    psum x1, waiting for transfers between devices, from_root(): return lax.psum(kept, axis)  146 us
    all_gather x1, waiting for transfers between devices, per_device(): row_block = lax.all_gather(factor, 'col', axis=0, tiled=True)  100 us
    dot_general x1, matrix products, per_device(): jnp.dot(inverse, panel, precision=lax.Precision.HIGHEST, preferred_elemen...  91.4 us
    psum x1, waiting for transfers between devices, per_device(): schur = lax.psum(schur_term, 'row')  50.2 us
  transfers between devices with their start and end apart: 4, of which 4 were waited for; matrix products, arithmetic and copies ran while one was open for 1% of the time, Pallas kernels for 0%

commit v1 on v0

v1 whole, which is shorter than its diff:
```python
import functools
import math

import jax
import jax.numpy as jnp
from jax import lax
from jax.experimental import pallas as pl
from jax.experimental.pallas import tpu as pltpu
from jax.sharding import PartitionSpec as P

MESH = pl.DeviceIdType.MESH


def membership(first_row, row_total, block_sizes, listed):
    block_ends = jnp.cumsum(block_sizes)
    block_starts = block_ends - block_sizes
    positions = first_row + jnp.arange(row_total, dtype=jnp.int32)
    inside = (
        (positions[:, None] >= block_starts[None, :]) & (positions[:, None] < block_ends[None, :])
    ).astype(jnp.float32)
    return jnp.dot(
        inside,
        listed.astype(jnp.float32).T,
        precision=lax.Precision.HIGHEST,
        preferred_element_type=jnp.float32,
    )


def holder(k, n_rowdev, n_coldev):
    ratio = n_rowdev // n_coldev
    part = k // n_coldev
    place = k % n_coldev
    return (place + (part % 2) * (n_coldev - 1 - 2 * place)) * ratio + part


def shard_of(row, n_rowdev, n_coldev):
    ratio = n_rowdev // n_coldev
    part = row % ratio
    place = row // ratio
    return part * n_coldev + place + (part % 2) * (n_coldev - 1 - 2 * place)


def flip(row, bit):
    return row + bit * (1 - 2 * ((row // bit) % 2))


def product_kernel(
    n_rowdev, n_coldev, parts, depth,
    own_ref, inverse_ref, out_ref,
    panel, high, low, tiles, sums, from_below, from_above,
    gather_send, gather_recv, tile_sem, sum_send, below_recv, above_recv,
):
    row = lax.axis_index("row")
    col = lax.axis_index("col")
    sibling_count, shard_rows, width = own_ref.shape
    col_rows = panel.shape[1]
    piece = shard_rows // parts
    bits = [1 << i for i in range(n_rowdev.bit_length() - 1)]

    number = row * n_coldev + col
    target_row = holder(number % n_rowdev, n_rowdev, n_coldev)
    target_col = number // n_rowdev
    source = col * n_rowdev + shard_of(row, n_rowdev, n_coldev)
    source_row = source // n_coldev
    source_col = source % n_coldev
    moving = target_row * n_coldev + target_col != number

    barrier = pltpu.get_barrier_semaphore()

    def greet(to_row, to_col):
        pl.semaphore_signal(barrier, inc=1, device_id=(to_row, to_col), device_id_type=MESH)

    for bit in bits:
        greet(flip(row, bit), col)

    @pl.when(moving)
    def _():
        greet(target_row, target_col)
        greet(source_row, source_col)

    @pl.when(col > 0)
    def _():
        greet(row, col - 1)

    @pl.when(col < n_coldev - 1)
    def _():
        greet(row, col + 1)

    pl.semaphore_wait(
        barrier,
        len(bits)
        + jnp.where(moving, 2, 0)
        + jnp.where(col > 0, 1, 0)
        + jnp.where(col < n_coldev - 1, 1, 0),
    )

    def place(of_row, part):
        start = shard_of(of_row, n_rowdev, n_coldev) * shard_rows + part * piece
        return pl.ds(pl.multiple_of(start, 8), piece)

    def orders(s):
        rest = bits[1:]
        return (rest if s % 2 else rest[::-1]) + bits[:1]

    def move(s, part):
        return pltpu.make_async_remote_copy(
            src_ref=own_ref.at[s, pl.ds(part * piece, piece)],
            dst_ref=panel.at[s, place(target_row, part)],
            send_sem=gather_send.at[s, part, 0],
            recv_sem=gather_recv.at[s, part, 0],
            device_id=(target_row, target_col),
            device_id_type=MESH,
        )

    def keep(s, part):
        return pltpu.make_async_copy(
            own_ref.at[s, pl.ds(part * piece, piece)],
            panel.at[s, place(row, part)],
            gather_recv.at[s, part, 0],
        )

    def exchanges(s, part, stage):
        order = orders(s)
        held = [row]
        for bit in order[:stage - 1]:
            held = held + [flip(r, bit) for r in held]
        partner = flip(row, order[stage - 1])
        copies = []
        for m, slot in enumerate(held):
            entry = (1 << (stage - 1)) + m
            where = panel.at[s, place(slot, part)]
            copies.append(pltpu.make_async_remote_copy(
                src_ref=where,
                dst_ref=where,
                send_sem=gather_send.at[s, part, entry],
                recv_sem=gather_recv.at[s, part, entry],
                device_id=(partner, col),
                device_id_type=MESH,
            ))
        return copies

    def start_stage(s, part, stage):
        if stage == 0:
            @pl.when(moving)
            def _():
                move(s, part).start()

            @pl.when(jnp.logical_not(moving))
            def _():
                keep(s, part).start()
        else:
            for copy in exchanges(s, part, stage):
                copy.start()

    def end_stage(s, part, stage):
        if stage == 0:
            @pl.when(moving)
            def _():
                move(s, part).wait_recv()

            @pl.when(jnp.logical_not(moving))
            def _():
                keep(s, part).wait()
        else:
            for copy in exchanges(s, part, stage):
                copy.wait_recv()

    items = [(s, part) for part in range(parts) for s in range(sibling_count)]
    for s, part in items:
        start_stage(s, part, 0)

    others = (n_coldev - 1) * parts
    total = n_coldev * parts
    swap = col > n_coldev - 1 - col
    near = jnp.where(swap, n_coldev - 1 - col, col)
    lead = n_coldev - 1 - 2 * near
    minor_total = near * parts

    def plan(t):
        inner = t - lead
        paired = jnp.logical_and(inner >= 0, inner < 2 * minor_total)
        minor = jnp.logical_and(paired, inner % 2 == 1)
        major_at = jnp.where(inner < 0, t, jnp.where(paired, lead + inner // 2, t - minor_total))
        index = jnp.where(minor, inner // 2, major_at)
        up = jnp.where(swap, minor, jnp.logical_not(minor))
        block = jnp.where(up, n_coldev - 1 - index // parts, index // parts)
        is_own = t >= others
        block = jnp.where(is_own, col, block)
        part = jnp.where(is_own, t - others, index % parts)
        up = jnp.logical_and(up, jnp.logical_not(is_own))
        down = jnp.logical_and(jnp.logical_not(up), jnp.logical_not(is_own))
        return block, part, up, down, is_own

    def load(t):
        block, part, _, _, _ = plan(t)
        start = pl.multiple_of(block * shard_rows + part * piece, 8)
        return pltpu.make_async_copy(
            inverse_ref.at[pl.ds(start, piece)], tiles.at[t % 2], tile_sem.at[t % 2]
        )

    load(0).start()

    stages = 1 + len(bits)
    for tick in range(parts + stages):
        for s, part in items:
            stage = tick - part
            if 0 <= stage < stages:
                end_stage(s, part, stage)
                if stage + 1 < stages:
                    start_stage(s, part, stage + 1)

    @pl.loop(0, col_rows // 256 if col_rows % 256 == 0 else 1)
    def _(i):
        step = 256 if col_rows % 256 == 0 else col_rows
        rows = pl.ds(pl.multiple_of(i * step, step), step)
        for s in range(sibling_count):
            value = panel[s, rows, :]
            top = value.astype(jnp.bfloat16)
            high[rows, s * width:(s + 1) * width] = top
            low[rows, s * width:(s + 1) * width] = (
                value - top.astype(jnp.float32)
            ).astype(jnp.bfloat16)

    def pass_up(block, part):
        return pltpu.make_async_remote_copy(
            src_ref=sums.at[block, part],
            dst_ref=from_below.at[block, part],
            send_sem=sum_send.at[block, part],
            recv_sem=below_recv.at[block, part],
            device_id=(row, col + 1),
            device_id_type=MESH,
        )

    def pass_down(block, part):
        return pltpu.make_async_remote_copy(
            src_ref=sums.at[block, part],
            dst_ref=from_above.at[block, part],
            send_sem=sum_send.at[block, part],
            recv_sem=above_recv.at[block, part],
            device_id=(row, col - 1),
            device_id_type=MESH,
        )

    @pl.loop(0, total)
    def _(t):
        block, part, up, down, is_own = plan(t)

        @pl.when(t + 1 < total)
        def _():
            load(t + 1).start()

        load(t).wait()
        sums[block, part] = jnp.zeros((piece, sibling_count * width), jnp.float32)

        @pl.loop(0, col_rows // depth)
        def _(k):
            span = pl.ds(pl.multiple_of(k * depth, depth), depth)
            value = tiles[t % 2, :, span]
            top = value.astype(jnp.bfloat16)
            rest = (value - top.astype(jnp.float32)).astype(jnp.bfloat16)
            dot = functools.partial(jnp.dot, preferred_element_type=jnp.float32)
            sums[block, part] += (
                dot(top, low[span, :]) + dot(rest, high[span, :]) + dot(top, high[span, :])
            )

        @pl.when(jnp.logical_and(jnp.logical_not(down), col > 0))
        def _():
            pass_up(block, part).wait_recv()
            sums[block, part] += from_below[block, part]

        @pl.when(jnp.logical_and(jnp.logical_not(up), col < n_coldev - 1))
        def _():
            pass_down(block, part).wait_recv()
            sums[block, part] += from_above[block, part]

        @pl.when(up)
        def _():
            pass_up(block, part).start()

        @pl.when(down)
        def _():
            pass_down(block, part).start()

        @pl.when(is_own)
        def _():
            out_ref[part] = sums[block, part]

    @pl.loop(0, others)
    def _(t):
        block, part, up, down, _ = plan(t)

        @pl.when(up)
        def _():
            pass_up(block, part).wait_send()

        @pl.when(down)
        def _():
            pass_down(block, part).wait_send()

    for s, part in items:
        @pl.when(moving)
        def _():
            move(s, part).wait_send()

        for stage in range(1, stages):
            for copy in exchanges(s, part, stage):
                copy.wait_send()


def product(n_rowdev, n_coldev, inverse, own):
    sibling_count, shard_rows, width = own.shape
    block_total, col_rows = inverse.shape
    parts = 2 if shard_rows % 16 == 0 else 1
    piece = shard_rows // parts
    depth = math.gcd(col_rows, 1280)
    columns = sibling_count * width
    f32 = jnp.float32
    vmem = pl.BlockSpec(memory_space=pltpu.VMEM)
    out = pl.pallas_call(
        functools.partial(product_kernel, n_rowdev, n_coldev, parts, depth),
        out_shape=jax.ShapeDtypeStruct((parts, piece, columns), f32),
        in_specs=[vmem, pl.BlockSpec(memory_space=pl.ANY)],
        out_specs=vmem,
        scratch_shapes=[
            pltpu.VMEM((sibling_count, col_rows, width), f32),
            pltpu.VMEM((col_rows, columns), jnp.bfloat16),
            pltpu.VMEM((col_rows, columns), jnp.bfloat16),
            pltpu.VMEM((2, piece, col_rows), f32),
            pltpu.VMEM((n_coldev, parts, piece, columns), f32),
            pltpu.VMEM((n_coldev, parts, piece, columns), f32),
            pltpu.VMEM((n_coldev, parts, piece, columns), f32),
            pltpu.SemaphoreType.DMA((sibling_count, parts, n_rowdev)),
            pltpu.SemaphoreType.DMA((sibling_count, parts, n_rowdev)),
            pltpu.SemaphoreType.DMA((2,)),
            pltpu.SemaphoreType.DMA((n_coldev, parts)),
            pltpu.SemaphoreType.DMA((n_coldev, parts)),
            pltpu.SemaphoreType.DMA((n_coldev, parts)),
        ],
        compiler_params=pltpu.CompilerParams(
            collective_id=0, has_side_effects=True, vmem_limit_bytes=60_000_000
        ),
        name="gather_product_scatter",
    )(own, inverse)
    return out.reshape(shard_rows, columns)


def total_kernel(
    n_rowdev, n_coldev, x_ref, out_ref,
    got, mine, gathered, whole, first_send, first_recv, second_send, second_recv,
    third_send, third_recv,
):
    row = lax.axis_index("row")
    col = lax.axis_index("col")
    barrier = pltpu.get_barrier_semaphore()
    for step in range(1, n_rowdev):
        pl.semaphore_signal(
            barrier, inc=1, device_id=((row + step) % n_rowdev, col), device_id_type=MESH
        )
    for step in range(1, n_coldev):
        pl.semaphore_signal(
            barrier, inc=1, device_id=(row, (col + step) % n_coldev), device_id_type=MESH
        )
    pl.semaphore_wait(barrier, n_rowdev + n_coldev - 2)

    def scatter(step):
        peer = (row + step) % n_rowdev
        return pltpu.make_async_remote_copy(
            src_ref=x_ref.at[peer], dst_ref=got.at[step],
            send_sem=first_send.at[step], recv_sem=first_recv.at[step],
            device_id=(peer, col), device_id_type=MESH,
        )

    def share(step):
        return pltpu.make_async_remote_copy(
            src_ref=mine, dst_ref=gathered.at[step],
            send_sem=second_send.at[step], recv_sem=second_recv.at[step],
            device_id=(row, (col + step) % n_coldev), device_id_type=MESH,
        )

    def spread(step):
        return pltpu.make_async_remote_copy(
            src_ref=whole, dst_ref=out_ref.at[row],
            send_sem=third_send.at[step], recv_sem=third_recv.at[step],
            device_id=((row + step) % n_rowdev, col), device_id_type=MESH,
        )

    for step in range(1, n_rowdev):
        scatter(step).start()
    value = x_ref[row]
    for step in range(1, n_rowdev):
        scatter(step).wait_recv()
        value = value + got[step]
    mine[...] = value
    for step in range(1, n_coldev):
        share(step).start()
    for step in range(1, n_coldev):
        share(step).wait_recv()
    gathered[0] = mine[...]
    value = gathered[col]
    for place in range(1, n_coldev):
        value = value + gathered[(col - place + n_coldev) % n_coldev]
    whole[...] = value
    for step in range(1, n_rowdev):
        spread(step).start()
    out_ref[row] = whole[...]
    for step in range(1, n_rowdev):
        spread(step).wait_recv()
    for step in range(1, n_rowdev):
        scatter(step).wait_send()
        spread(step).wait_send()
    for step in range(1, n_coldev):
        share(step).wait_send()


def total(n_rowdev, n_coldev, value):
    rows, columns = value.shape
    piece = rows // n_rowdev
    vmem = pl.BlockSpec(memory_space=pltpu.VMEM)
    dma = pltpu.SemaphoreType.DMA
    out = pl.pallas_call(
        functools.partial(total_kernel, n_rowdev, n_coldev),
        out_shape=jax.ShapeDtypeStruct((n_rowdev, piece, columns), jnp.float32),
        in_specs=[vmem],
        out_specs=vmem,
        scratch_shapes=[
            pltpu.VMEM((n_rowdev, piece, columns), jnp.float32),
            pltpu.VMEM((piece, columns), jnp.float32),
            pltpu.VMEM((n_coldev, piece, columns), jnp.float32),
            pltpu.VMEM((piece, columns), jnp.float32),
            dma((n_rowdev,)), dma((n_rowdev,)), dma((n_coldev,)), dma((n_coldev,)),
            dma((n_rowdev,)), dma((n_rowdev,)),
        ],
        compiler_params=pltpu.CompilerParams(collective_id=1, has_side_effects=True),
        name="schur_total",
    )(value.reshape(n_rowdev, piece, columns))
    return out.reshape(rows, columns)


def per_device(inverse, factor, diag_inverse, block_sizes, listed):
    n_rowdev = lax.axis_size("row")
    n_coldev = lax.axis_size("col")
    row_place = lax.axis_index("row")
    col_place = lax.axis_index("col")
    shard_rows, sibling_count, width = factor.shape

    member = membership(
        (row_place * n_coldev + col_place) * shard_rows, shard_rows, block_sizes, listed
    )
    own = jnp.transpose(factor, (1, 0, 2))
    summed = product(n_rowdev, n_coldev, inverse, own * member.T[:, :, None])
    results = [
        -(summed[:, s * width:(s + 1) * width] * member[:, s:s + 1])
        for s in range(sibling_count)
    ]
    terms = [
        lax.dot_general(
            own[s], results[s], (((0,), (0,)), ((), ())),
            precision=lax.Precision.HIGHEST, preferred_element_type=jnp.float32,
        )
        for s in range(sibling_count)
    ]
    schur = total(n_rowdev, n_coldev, jnp.concatenate(terms, axis=0))
    schur = schur.reshape(sibling_count, width, width)
    ancestor_rows = jnp.stack(results, axis=1)
    return (ancestor_rows, diag_inverse - schur)


def solution(mesh):
    in_specs = (P("row", "col"), P(("row", "col"), None, None), P(), P(), P())
    out_specs = (P(("row", "col"), None, None), P())
    return jax.shard_map(
        per_device, mesh=mesh, in_specs=in_specs, out_specs=out_specs, check_vma=False
    )
```

time: 655 us -> 257 us (0.39)
  waiting for transfers between devices: 485 us -> 0 us
  Pallas kernels: 0 us -> 241 us
  matrix products: 104 us -> 3.71 us
  local copies, waits for them, and re-layouts: 35.2 us -> 4.16 us
  between operations: 13.9 us -> 0.73 us
  other arithmetic: 14.1 us -> 6.54 us
    psum x3 -> x0, waiting for transfers between devices: 384 us -> none  [the longest x1 188 us: per_device(): summed = lax.psum(partial_value, 'col')]
    pallas_call x0 -> x2, Pallas kernels: none -> 241 us  [the longest x1 215 us: product(): pl.pallas_call(functools.partial(product_kernel, n_rowdev, n_coldev, part...]
    all_gather x1 -> x0, waiting for transfers between devices: 100 us -> none  [per_device(): row_block = lax.all_gather(factor, 'col', axis=0, tiled=True)]
    dot_general x2, matrix products: 103 us -> 2.68 us  [per_device(): lax.dot_general(own[s], results[s], (((0,), (0,)), ((), ())), precision=l...]
    select_n x2 -> x0, local copies, waits for them, and re-layouts: 11.8 us -> none  [from_root(): jnp.where(lax.axis_index(axis) == source, value, 0).astype(value.dtype)]
    reshape x1 -> x0, local copies, waits for them, and re-layouts: 8.72 us -> none  [per_device(): summed.reshape(block_total, sibling_count, width) * block_member[:, :, None]]
    select_n x1 -> x0, other arithmetic: 7.2 us -> none  [from_root(): jnp.where(lax.axis_index(axis) == source, value, 0).astype(value.dtype)]
  transfers between devices with their start and end apart: 4 -> 0, of which waited for: 4 -> 0; matrix products, arithmetic and copies ran while one was open for 1% -> 0% of each run, Pallas kernels for 0% -> 0%
where the time goes in v1:
time: 257 us
  Pallas kernels  241 us (94%)
  other arithmetic  6.54 us (3%)
  local copies, waits for them, and re-layouts  4.16 us (2%)
  matrix products  3.71 us (1%)
    pallas_call x1, Pallas kernels, product(): pl.pallas_call(functools.partial(product_kernel, n_rowdev, n_coldev, part...  215 us
    pallas_call x1, Pallas kernels, total(): pl.pallas_call(functools.partial(total_kernel, n_rowdev, n_coldev), out_s...  26.3 us

profile of v1, /device:TPU:1, one launch (start us, length us, event | category | flops | bytes accessed | tf_op | source)
XLA Modules:
  0.0 256.5 jit_solution(15991247091466340781)
XLA Ops:
  0.6 0.7 copy.11
  1.4 0.1 reduce-window.8
  1.5 0.1 reduce
  1.6 0.7 sub.6
  2.3 1.0 fusion.8
  3.3 2.6 %broadcast_multiply_fusion.own_ref = f32[2,640,256]{2,1,0:T(8,128)} fusion(f32[2,640]{1,0:T(2,128)S(1)} %bitcast.33, f32[640,2,256]{2,1,0:T(2,128)} %param.6), kind=kLoop, calls=%fused_computation.10 | loop fusion | flops 327680 | bytes 2626560 | tf_op jit(solution)/shard_map/mul | solution.py:450
  6.0 0.0 copy-start.1
  6.0 215.0 %gather_product_scatter.1 = f32[2,320,512]{2,1,0:T(8,128)} custom-call(f32[2,640,256]{2,1,0:T(8,128)} %broadcast_multiply_fusion.own_ref, f32[2560,5120]{1,0:T(8,128)} %inverse_ref.1), custom_call_target="tpu_custom_call" | custom-call | tf_op jit(solution)/shard_map/gather_product_scatter/pallas_call | solution.py:319
  221.0 0.0 copy-done.1
  221.0 0.0 copy-start
  221.0 0.1 copy.16
  221.1 1.2 copy-done
  222.3 1.3 convolution_bitcast_fusion.1
  223.7 1.3 convolution_bitcast_fusion
  225.0 0.2 fusion.3
  225.3 0.1 pad_maximum_fusion
  225.4 2.1 copy.12
  227.4 0.0 copy-start.2
  227.4 0.8 pad_maximum_fusion.1
  228.3 26.3 %schur_total.1 = f32[8,64,256]{2,1,0:T(8,128)} custom-call(f32[8,64,256]{2,1,0:T(8,128)} %bitcast.32), custom_call_target="tpu_custom_call" | custom-call | tf_op jit(solution)/shard_map/schur_total/pallas_call | solution.py:420
  254.6 0.0 copy-done.2
  254.6 1.9 bitcast_subtract_fusion
  (2 shorter events, 0.0 us)
Async XLA Ops:
  6.0 215.1 %copy-start.1 = (f32[640,2,256]{2,1,0:T(2,128)S(1)}, f32[640,2,256]{2,1,0:T(2,128)}, u32[]{:S(2)}) copy-start(f32[640,2,256]{2,1,0:T(2,128)} %param.6) | copy-start | bytes 3932164
  221.0 1.3 copy-start
  227.4 27.2 %copy-start.2 = (f32[2,256,256]{2,1,0:T(8,128)S(1)}, f32[2,256,256]{2,1,0:T(8,128)}, u32[]{:S(2)}) copy-start(f32[2,256,256]{2,1,0:T(8,128)} %param.7) | copy-start | bytes 1572868

commit v2 on v1

--- a/solution.py
+++ b/solution.py
@@ -98,9 +98,9 @@
         start = shard_of(of_row, n_rowdev, n_coldev) * shard_rows + part * piece
         return pl.ds(pl.multiple_of(start, 8), piece)
 
-    def orders(s):
+    def orders(part):
         rest = bits[1:]
-        return (rest if s % 2 else rest[::-1]) + bits[:1]
+        return (rest if part % 2 else rest[::-1]) + bits[:1]
 
     def move(s, part):
         return pltpu.make_async_remote_copy(
@@ -120,7 +120,7 @@
         )
 
     def exchanges(s, part, stage):
-        order = orders(s)
+        order = orders(part)
         held = [row]
         for bit in order[:stage - 1]:
             held = held + [flip(r, bit) for r in held]
@@ -165,7 +165,7 @@
             for copy in exchanges(s, part, stage):
                 copy.wait_recv()
 
-    items = [(s, part) for part in range(parts) for s in range(sibling_count)]
+    items = [(s, part) for s in range(sibling_count) for part in range(parts)]
     for s, part in items:
         start_stage(s, part, 0)
 
@@ -191,111 +191,138 @@
         down = jnp.logical_and(jnp.logical_not(up), jnp.logical_not(is_own))
         return block, part, up, down, is_own
 
-    def load(t):
-        block, part, _, _, _ = plan(t)
+    def load(s, t):
+        block, part, _, _, _ = plan(t % total)
         start = pl.multiple_of(block * shard_rows + part * piece, 8)
+        slot = (s * total + t) % 2
         return pltpu.make_async_copy(
-            inverse_ref.at[pl.ds(start, piece)], tiles.at[t % 2], tile_sem.at[t % 2]
-        )
-
-    load(0).start()
+            inverse_ref.at[pl.ds(start, piece)], tiles.at[slot], tile_sem.at[slot]
+        )
+
+    load(0, 0).start()
 
     stages = 1 + len(bits)
     for tick in range(parts + stages):
-        for s, part in items:
+        for part in range(parts):
             stage = tick - part
             if 0 <= stage < stages:
-                end_stage(s, part, stage)
+                end_stage(0, part, stage)
                 if stage + 1 < stages:
-                    start_stage(s, part, stage + 1)
-
-    @pl.loop(0, col_rows // 256 if col_rows % 256 == 0 else 1)
-    def _(i):
-        step = 256 if col_rows % 256 == 0 else col_rows
-        rows = pl.ds(pl.multiple_of(i * step, step), step)
-        for s in range(sibling_count):
+                    start_stage(0, part, stage + 1)
+
+    step = math.gcd(col_rows, 256)
+
+    def split(s):
+        @pl.loop(0, col_rows // step)
+        def _(i):
+            rows = pl.ds(pl.multiple_of(i * step, step), step)
             value = panel[s, rows, :]
             top = value.astype(jnp.bfloat16)
-            high[rows, s * width:(s + 1) * width] = top
-            low[rows, s * width:(s + 1) * width] = (
-                value - top.astype(jnp.float32)
-            ).astype(jnp.bfloat16)
-
-    def pass_up(block, part):
-        return pltpu.make_async_remote_copy(
-            src_ref=sums.at[block, part],
-            dst_ref=from_below.at[block, part],
-            send_sem=sum_send.at[block, part],
-            recv_sem=below_recv.at[block, part],
+            high[s, rows, :] = top
+            low[s, rows, :] = (value - top.astype(jnp.float32)).astype(jnp.bfloat16)
+
+    def pass_up(s, block, part):
+        return pltpu.make_async_remote_copy(
+            src_ref=sums.at[s, block, part],
+            dst_ref=from_below.at[s, block, part],
+            send_sem=sum_send.at[s, block, part],
+            recv_sem=below_recv.at[s, block, part],
             device_id=(row, col + 1),
             device_id_type=MESH,
         )
 
-    def pass_down(block, part):
-        return pltpu.make_async_remote_copy(
-            src_ref=sums.at[block, part],
-            dst_ref=from_above.at[block, part],
-            send_sem=sum_send.at[block, part],
-            recv_sem=above_recv.at[block, part],
+    def pass_down(s, block, part):
+        return pltpu.make_async_remote_copy(
+            src_ref=sums.at[s, block, part],
+            dst_ref=from_above.at[s, block, part],
+            send_sem=sum_send.at[s, block, part],
+            recv_sem=above_recv.at[s, block, part],
             device_id=(row, col - 1),
             device_id_type=MESH,
         )
 
-    @pl.loop(0, total)
-    def _(t):
-        block, part, up, down, is_own = plan(t)
-
-        @pl.when(t + 1 < total)
-        def _():
-            load(t + 1).start()
-
-        load(t).wait()
-        sums[block, part] = jnp.zeros((piece, sibling_count * width), jnp.float32)
-
-        @pl.loop(0, col_rows // depth)
-        def _(k):
-            span = pl.ds(pl.multiple_of(k * depth, depth), depth)
-            value = tiles[t % 2, :, span]
-            top = value.astype(jnp.bfloat16)
-            rest = (value - top.astype(jnp.float32)).astype(jnp.bfloat16)
-            dot = functools.partial(jnp.dot, preferred_element_type=jnp.float32)
-            sums[block, part] += (
-                dot(top, low[span, :]) + dot(rest, high[span, :]) + dot(top, high[span, :])
-            )
-
-        @pl.when(jnp.logical_and(jnp.logical_not(down), col > 0))
-        def _():
-            pass_up(block, part).wait_recv()
-            sums[block, part] += from_below[block, part]
-
-        @pl.when(jnp.logical_and(jnp.logical_not(up), col < n_coldev - 1))
-        def _():
-            pass_down(block, part).wait_recv()
-            sums[block, part] += from_above[block, part]
-
-        @pl.when(up)
-        def _():
-            pass_up(block, part).start()
-
-        @pl.when(down)
-        def _():
-            pass_down(block, part).start()
-
-        @pl.when(is_own)
-        def _():
-            out_ref[part] = sums[block, part]
-
-    @pl.loop(0, others)
-    def _(t):
-        block, part, up, down, _ = plan(t)
-
-        @pl.when(up)
-        def _():
-            pass_up(block, part).wait_send()
-
-        @pl.when(down)
-        def _():
-            pass_down(block, part).wait_send()
+    hooks = [(stage, part) for stage in range(stages - 1) for part in range(parts)]
+
+    def advance(s, hook):
+        stage, part = hook
+        end_stage(s, part, stage)
+        start_stage(s, part, stage + 1)
+
+    for s in range(sibling_count):
+        split(s)
+        follows = s + 1 < sibling_count
+
+        @pl.loop(0, total)
+        def _(t):
+            block, part, up, down, is_own = plan(t)
+            slot = (s * total + t) % 2
+
+            @pl.when(t + 1 < (total + 1 if follows else total))
+            def _():
+                load(s, t + 1).start()
+
+            load(s, t).wait()
+            sums[s, block, part] = jnp.zeros((piece, width), jnp.float32)
+
+            @pl.loop(0, col_rows // depth)
+            def _(k):
+                span = pl.ds(pl.multiple_of(k * depth, depth), depth)
+                value = tiles[slot, :, span]
+                top = value.astype(jnp.bfloat16)
+                rest = (value - top.astype(jnp.float32)).astype(jnp.bfloat16)
+                dot = functools.partial(jnp.dot, preferred_element_type=jnp.float32)
+                sums[s, block, part] += (
+                    dot(top, low[s, span, :])
+                    + dot(rest, high[s, span, :])
+                    + dot(top, high[s, span, :])
+                )
+
+            @pl.when(jnp.logical_and(jnp.logical_not(down), col > 0))
+            def _():
+                pass_up(s, block, part).wait_recv()
+                sums[s, block, part] += from_below[s, block, part]
+
+            @pl.when(jnp.logical_and(jnp.logical_not(up), col < n_coldev - 1))
+            def _():
+                pass_down(s, block, part).wait_recv()
+                sums[s, block, part] += from_above[s, block, part]
+
+            @pl.when(up)
+            def _():
+                pass_up(s, block, part).start()
+
+            @pl.when(down)
+            def _():
+                pass_down(s, block, part).start()
+
+            @pl.when(is_own)
+            def _():
+                out_ref[s, part] = sums[s, block, part]
+
+            if follows:
+                for at, hook in enumerate(hooks[:total]):
+                    @pl.when(t == at)
+                    def _(hook=hook):
+                        advance(s + 1, hook)
+
+        if follows:
+            for hook in hooks[total:]:
+                advance(s + 1, hook)
+            for part in range(parts):
+                end_stage(s + 1, part, stages - 1)
+
+    for s in range(sibling_count):
+        @pl.loop(0, others)
+        def _(t):
+            block, part, up, down, _ = plan(t)
+
+            @pl.when(up)
+            def _():
+                pass_up(s, block, part).wait_send()
+
+            @pl.when(down)
+            def _():
+                pass_down(s, block, part).wait_send()
 
     for s, part in items:
         @pl.when(moving)
@@ -313,35 +340,34 @@
     parts = 2 if shard_rows % 16 == 0 else 1
     piece = shard_rows // parts
     depth = math.gcd(col_rows, 1280)
-    columns = sibling_count * width
     f32 = jnp.float32
     vmem = pl.BlockSpec(memory_space=pltpu.VMEM)
     out = pl.pallas_call(
         functools.partial(product_kernel, n_rowdev, n_coldev, parts, depth),
-        out_shape=jax.ShapeDtypeStruct((parts, piece, columns), f32),
+        out_shape=jax.ShapeDtypeStruct((sibling_count, parts, piece, width), f32),
         in_specs=[vmem, pl.BlockSpec(memory_space=pl.ANY)],
         out_specs=vmem,
         scratch_shapes=[
             pltpu.VMEM((sibling_count, col_rows, width), f32),
-            pltpu.VMEM((col_rows, columns), jnp.bfloat16),
-            pltpu.VMEM((col_rows, columns), jnp.bfloat16),
+            pltpu.VMEM((sibling_count, col_rows, width), jnp.bfloat16),
+            pltpu.VMEM((sibling_count, col_rows, width), jnp.bfloat16),
             pltpu.VMEM((2, piece, col_rows), f32),
-            pltpu.VMEM((n_coldev, parts, piece, columns), f32),
-            pltpu.VMEM((n_coldev, parts, piece, columns), f32),
-            pltpu.VMEM((n_coldev, parts, piece, columns), f32),
+            pltpu.VMEM((sibling_count, n_coldev, parts, piece, width), f32),
+            pltpu.VMEM((sibling_count, n_coldev, parts, piece, width), f32),
+            pltpu.VMEM((sibling_count, n_coldev, parts, piece, width), f32),
             pltpu.SemaphoreType.DMA((sibling_count, parts, n_rowdev)),
             pltpu.SemaphoreType.DMA((sibling_count, parts, n_rowdev)),
             pltpu.SemaphoreType.DMA((2,)),
-            pltpu.SemaphoreType.DMA((n_coldev, parts)),
-            pltpu.SemaphoreType.DMA((n_coldev, parts)),
-            pltpu.SemaphoreType.DMA((n_coldev, parts)),
+            pltpu.SemaphoreType.DMA((sibling_count, n_coldev, parts)),
+            pltpu.SemaphoreType.DMA((sibling_count, n_coldev, parts)),
+            pltpu.SemaphoreType.DMA((sibling_count, n_coldev, parts)),
         ],
         compiler_params=pltpu.CompilerParams(
             collective_id=0, has_side_effects=True, vmem_limit_bytes=60_000_000
         ),
         name="gather_product_scatter",
     )(own, inverse)
-    return out.reshape(shard_rows, columns)
+    return out.reshape(sibling_count, shard_rows, width)
 
 
 def total_kernel(
@@ -449,7 +475,7 @@
     own = jnp.transpose(factor, (1, 0, 2))
     summed = product(n_rowdev, n_coldev, inverse, own * member.T[:, :, None])
     results = [
-        -(summed[:, s * width:(s + 1) * width] * member[:, s:s + 1])
+        -(summed[s] * member[:, s:s + 1])
         for s in range(sibling_count)
     ]
     terms = [

time: 257 us -> 237 us (0.922)
  Pallas kernels: 241 us -> 221 us
    pallas_call x1, Pallas kernels: 215 us -> 187 us  [product(): pl.pallas_call(functools.partial(product_kernel, n_rowdev, n_coldev, part...]
    pallas_call x1, Pallas kernels: 26.3 us -> 33.6 us  [total(): pl.pallas_call(functools.partial(total_kernel, n_rowdev, n_coldev), out_s...]
where the time goes in v2:
time: 237 us; the launch traced here: 236 us
  Pallas kernels  221 us (93%)
  other arithmetic  8.08 us (3%)
  matrix products  3.5 us (1%)
  local copies, waits for them, and re-layouts  3.11 us (1%)
    pallas_call x1, Pallas kernels, product(): pl.pallas_call(functools.partial(product_kernel, n_rowdev, n_coldev, part...  187 us
    pallas_call x1, Pallas kernels, total(): pl.pallas_call(functools.partial(total_kernel, n_rowdev, n_coldev), out_s...  33.6 us

profile of v2, /device:TPU:1, one launch (start us, length us, event | category | flops | bytes accessed | tf_op | source)
XLA Modules:
  0.0 236.4 jit_solution(13905035893668347605)
XLA Ops:
  0.6 0.7 copy.16
  1.4 0.1 reduce-window.8
  1.5 0.1 reduce
  1.6 0.7 sub.6
  2.3 1.0 fusion.2
  3.3 0.1 mul.66
  3.4 0.1 mul.69
  3.5 2.6 %broadcast_multiply_fusion.own_ref = f32[2,640,256]{2,1,0:T(8,128)} fusion(f32[2,640]{1,0:T(2,128)S(1)} %bitcast.39, f32[640,2,256]{2,1,0:T(2,128)} %param.6), kind=kLoop, calls=%fused_computation.12 | loop fusion | flops 327680 | bytes 2626560 | tf_op jit(solution)/shard_map/mul | solution.py:476
  6.1 187.4 %gather_product_scatter.1 = f32[2,2,320,256]{3,2,1,0:T(8,128)} custom-call(f32[2,640,256]{2,1,0:T(8,128)} %broadcast_multiply_fusion.own_ref, f32[2560,5120]{1,0:T(8,128)} %inverse_ref.1), custom_call_target="tpu_custom_call" | custom-call | tf_op jit(solution)/shard_map/gather_product_scatter/pallas_call | solution.py:345
  193.5 1.5 multiply_negate_fusion.1
  195.1 0.2 fusion
  195.3 0.1 pad_maximum_fusion
  195.4 0.0 copy-start
  195.4 2.1 copy.17
  197.5 0.0 copy-done
  197.5 0.1 copy.21
  197.6 1.2 convolution_bitcast_fusion.1
  198.8 1.2 convolution_bitcast_fusion
  200.1 0.0 copy-start.1
  200.1 0.8 pad_maximum_fusion.1
  200.9 33.6 %schur_total.1 = f32[8,64,256]{2,1,0:T(8,128)} custom-call(f32[8,64,256]{2,1,0:T(8,128)} %bitcast.38), custom_call_target="tpu_custom_call" | custom-call | tf_op jit(solution)/shard_map/schur_total/pallas_call | solution.py:446
  234.5 0.0 copy-done.1
  234.5 1.9 bitcast_subtract_fusion
  (2 shorter events, 0.0 us)
Async XLA Ops:
  195.4 2.1 copy-start
  200.1 34.4 %copy-start.1 = (f32[2,256,256]{2,1,0:T(8,128)S(1)}, f32[2,256,256]{2,1,0:T(8,128)}, u32[]{:S(2)}) copy-start(f32[2,256,256]{2,1,0:T(8,128)} %param.7) | copy-start | bytes 1572868
